TPU v7x, 32 devices: a whole 2x2x4 slice. The times are simulated.
32 devices in a mesh: ctx: 8 (over y, x, core), tp: 4 (over z).
Axes of the slice: x: 2, y: 2, z: 4, core: 2. Of those that a mesh axis runs over, the one named last changes fastest.
Arguments:
- tokens: bfloat16 [4096, 4096], P('ctx', 'tp'), may hold values from -6 to 6
- norm_gain: float32 [4096], replicated, may hold values from 0.5 to 1.5
- proj_weight: bfloat16 [3, 4096, 2048], P(None, None, 'tp'), may hold values from -0.09375 to 0.09375
- short_taps: float32 [3, 3, 2048], P(None, None, 'tp'), may hold values from -1 to 1
- long_filter: float32 [4096, 2048], P('ctx', 'tp'), may hold values from -0.09375 to 0.09375
- skip_gain: float32 [2048], P('tp'), may hold values from -1 to 1
Outputs:
- output: bfloat16 [4096, 2048], P('ctx', 'tp')
All inputs are finite; a program needn't handle non-finite values.
Results may differ from a plain program's by a relative error of at most 0.0081.
Values may be sent and summed in bfloat16 or wider, within the bound.
A program may use at most 128 MiB of HBM per device.

v0:
```python
import math
import jax
import jax.numpy as jnp
from jax import lax
from jax.sharding import PartitionSpec as P

highest = lax.Precision.HIGHEST


def from_behind(array, axis, by):
    devices = lax.axis_size(axis)
    pairs = [(i, i + by) for i in range(devices) if 0 <= i + by < devices]
    return lax.ppermute(array, axis, pairs)


def outer_tables(part_count):
    frequency = jnp.arange(2 * part_count, dtype=jnp.int32)
    source = jnp.arange(part_count, dtype=jnp.int32)
    turn_count = frequency[:, None] * source[None, :] % (2 * part_count)
    angles = turn_count.astype(jnp.float32) * (math.pi / part_count)
    return (jnp.cos(angles), jnp.sin(angles))


def inner_tables(row_count):
    step_index = jnp.arange(row_count, dtype=jnp.int32)
    turn_count = step_index[:, None] * step_index[None, :] % row_count
    angles = turn_count.astype(jnp.float32) * (2.0 * math.pi / row_count)
    return (jnp.cos(angles), jnp.sin(angles))


def twist_tables(own_index, part_count, block_rows, total_length):
    frequency = jnp.arange(2 * part_count, dtype=jnp.int32)
    column = own_index * block_rows + jnp.arange(block_rows, dtype=jnp.int32)
    turn_count = frequency[:, None] * column[None, :] % total_length
    angles = turn_count.astype(jnp.float32) * (2.0 * math.pi / total_length)
    return (jnp.cos(angles)[:, :, None], jnp.sin(angles)[:, :, None])


def forward_transform(signal, part_count, tables, regroup, spread):
    outer_cos, outer_sin, inner_cos, inner_sin, twist_cos, twist_sin = tables
    row_count, width_all = signal.shape
    block_rows = row_count // part_count
    regrouped = regroup(signal).reshape(part_count, block_rows, width_all)
    outer_real = jnp.einsum("an,njw->ajw", outer_cos, regrouped, precision=highest)
    outer_imag = -jnp.einsum("an,njw->ajw", outer_sin, regrouped, precision=highest)
    turned_real = outer_real * twist_cos + outer_imag * twist_sin
    turned_imag = outer_imag * twist_cos - outer_real * twist_sin
    arrived = spread(jnp.stack([turned_real, turned_imag]))
    spec_real = jnp.einsum("bj,ejw->ebw", inner_cos, arrived[0], precision=highest) + jnp.einsum(
        "bj,ejw->ebw", inner_sin, arrived[1], precision=highest
    )
    spec_imag = jnp.einsum("bj,ejw->ebw", inner_cos, arrived[1], precision=highest) - jnp.einsum(
        "bj,ejw->ebw", inner_sin, arrived[0], precision=highest
    )
    return (spec_real, spec_imag)


def inverse_transform(spec_real, spec_imag, part_count, tables):
    outer_cos, outer_sin, inner_cos, inner_sin, twist_cos, twist_sin = tables
    row_count = spec_real.shape[1]
    width_all = spec_real.shape[2]
    back_real = jnp.einsum("jb,ebw->ejw", inner_cos, spec_real, precision=highest) - jnp.einsum(
        "jb,ebw->ejw", inner_sin, spec_imag, precision=highest
    )
    back_imag = jnp.einsum("jb,ebw->ejw", inner_sin, spec_real, precision=highest) + jnp.einsum(
        "jb,ebw->ejw", inner_cos, spec_imag, precision=highest
    )
    arrived = lax.all_to_all(
        jnp.stack([back_real, back_imag]), "ctx", split_axis=2, concat_axis=1, tiled=True
    )
    turned_real = arrived[0] * twist_cos - arrived[1] * twist_sin
    turned_imag = arrived[0] * twist_sin + arrived[1] * twist_cos
    total_length = 2 * row_count * part_count
    folded = (
        jnp.einsum("an,ajw->njw", outer_cos, turned_real, precision=highest)
        - jnp.einsum("an,ajw->njw", outer_sin, turned_imag, precision=highest)
    ) / total_length
    return lax.all_to_all(
        folded.reshape(row_count, width_all), "ctx", split_axis=0, concat_axis=0, tiled=True
    )


def body(tokens, norm_gain, proj_weight, short_taps, long_filter, skip_gain):
    gathered = lax.all_gather(tokens, "tp", axis=1, tiled=True)
    widened = gathered.astype(jnp.float32)
    scaling = lax.rsqrt(jnp.mean(widened * widened, axis=1, keepdims=True) + 1e-06)
    normed = (widened * scaling * norm_gain).astype(jnp.bfloat16)
    projected = jnp.einsum(
        "td,bdc->btc", normed, proj_weight, preferred_element_type=jnp.float32
    ).astype(jnp.bfloat16)
    previous = from_behind(projected[:, -2:, :], "ctx", 1)
    extended = jnp.concatenate([previous, projected], axis=1).astype(jnp.float32)
    branch = (
        short_taps[:, 0, None, :] * extended[:, 2:, :]
        + short_taps[:, 1, None, :] * extended[:, 1:-1, :]
        + short_taps[:, 2, None, :] * extended[:, :-2, :]
    )
    mixed_field = branch[1] * branch[2]
    row_count, channels = mixed_field.shape
    part_count = lax.axis_size("ctx")
    own_index = lax.axis_index("ctx")
    block_rows = row_count // part_count
    total_length = 2 * row_count * part_count
    outer_cos, outer_sin = outer_tables(part_count)
    inner_cos, inner_sin = inner_tables(row_count)
    twist_cos, twist_sin = twist_tables(own_index, part_count, block_rows, total_length)
    tables = (outer_cos, outer_sin, inner_cos, inner_sin, twist_cos, twist_sin)
    gain_real, gain_imag = forward_transform(
        long_filter,
        part_count,
        tables,
        lambda values: lax.all_to_all(values, "ctx", split_axis=0, concat_axis=0, tiled=True),
        lambda values: lax.all_to_all(
            values.astype(jnp.bfloat16), "ctx", split_axis=1, concat_axis=2, tiled=True
        ).astype(values.dtype),
    )
    data_real, data_imag = forward_transform(
        mixed_field,
        part_count,
        tables,
        lambda values: lax.all_to_all(values, "ctx", split_axis=0, concat_axis=0, tiled=True),
        lambda values: lax.all_to_all(
            values.astype(jnp.bfloat16), "ctx", split_axis=1, concat_axis=2, tiled=True
        ).astype(values.dtype),
    )
    product_real = data_real * gain_real - data_imag * gain_imag
    product_imag = data_real * gain_imag + data_imag * gain_real
    convolved = inverse_transform(product_real, product_imag, part_count, tables)
    return (branch[0] * (convolved + skip_gain * mixed_field)).astype(jnp.bfloat16)


def solution(mesh):
    placed = (
        P("ctx", "tp"),
        P(),
        P(None, None, "tp"),
        P(None, None, "tp"),
        P("ctx", "tp"),
        P("tp"),
    )
    return jax.shard_map(
        body, mesh=mesh, in_specs=placed, out_specs=P("ctx", "tp"), check_vma=False
    )
```

profile of v0, /device:TPU:0, one launch (start us, length us, event | category | flops | bytes accessed | tf_op | source)
XLA Modules:
  0.0 390.0 jit_solution(1918648023505237398)
XLA Ops:
  6.5 0.0 all-gather.2.cloned.1.call-start
  6.5 0.7 all-gather.2.cloned.1.call-update
  7.3 5.2 %all-to-all-start.2 = ((f32[8,64,512]{2,1,0:T(8,128)}), f32[8,64,512]{2,1,0:T(8,128)}, u32[]{:S(2)}, u32[]{:S(2)}) async-start(f32[8,64,512]{2,1,0:T(8,128)} %bitcast.138), calls=%async_computation.2 | async-start | bytes 2097152 | tf_op jit(solution)/shard_map/all_to_all | solution.py:112
  12.4 0.0 copy-start.8
  12.5 79.9 %all-gather.2.cloned.1.call-done = bf16[512,4096]{1,0:T(8,128)(2,1)} async-done(((bf16[512,1024]{1,0:T(8,128)(2,1)}), bf16[512,4096]{1,0:T(8,128)(2,1)}) %all-gather.2.cloned.1.call-update) | async-done | bytes 4194320 | tf_op jit(solution)/shard_map/all_gather | solution.py:84
  92.4 3.2 fusion
  95.7 0.2 copy-done.3
  95.9 9.9 %fusion.33 = bf16[3,512,512]{2,1,0:T(8,128)(2,1)S(1)} fusion(bf16[3,4096,512]{2,1,0:T(8,128)(2,1)} %param.8, bf16[512,4096]{1,0:T(8,128)(2,1)S(1)} %copy-done.3, f32[4096]{0:T(1024)S(1)} %copy-done.8, f32[512]{0:T(512)S(1)} %add_rsqrt_fusion), kind=kOutput, calls=%fused_computation.50 | convolution fusion | flops 6451625984 | bytes 18368512 | tf_op jit(solution)/shard_map/td,bdc->btc/dot_general | solution.py:88
  105.8 1.8 collective-permute-start
  107.6 0.8 collective-permute-done
  108.3 0.5 maximum_convert_fusion
  108.8 0.9 fusion.8
  109.8 1.2 slice_multiply_fusion.3
  110.9 0.0 all-to-all-done.2
  110.9 6.6 %all-to-all-start = ((f32[8,64,512]{2,1,0:T(8,128)}), f32[8,64,512]{2,1,0:T(8,128)}, u32[]{:S(2)}, u32[]{:S(2)}) async-start(f32[8,64,512]{2,1,0:T(8,128)} %bitcast.135), calls=%async_computation | async-start | bytes 2097152 | tf_op jit(solution)/shard_map/all_to_all | solution.py:121
  117.5 0.2 fusion.104
  117.7 4.7 %fusion.75 = f32[16,64,512]{2,0,1:T(8,128)} fusion(f32[8,64,512]{2,1,0:T(8,128)} %all-to-all-done.2), kind=kOutput, calls=%fused_computation.89 | convolution fusion | flops 50333440 | bytes 3145728 | tf_op jit(solution)/shard_map/an,njw->ajw/dot_general | solution.py:45
  122.5 4.8 %fusion.77 = f32[16,64,512]{2,0,1:T(8,128)} fusion(f32[8,64,512]{2,1,0:T(8,128)} %all-to-all-done.2), kind=kOutput, calls=%fused_computation.91 | convolution fusion | flops 50333440 | bytes 3145728 | tf_op jit(solution)/shard_map/an,njw->ajw/dot_general | solution.py:44
  127.2 5.7 %all-to-all-done = f32[8,64,512]{2,1,0:T(8,128)} async-done(((f32[8,64,512]{2,1,0:T(8,128)}), f32[8,64,512]{2,1,0:T(8,128)}, u32[]{:S(2)}, u32[]{:S(2)}) %all-to-all-start) | async-done | bytes 1048608 | tf_op jit(solution)/shard_map/all_to_all | solution.py:121
  132.9 3.6 fusion.79
  136.5 5.9 %fusion.47 = (bf16[1,16,64,512]{3,1,2,0:T(8,128)(2,1)S(1)}, bf16[1,16,64,512]{3,1,2,0:T(8,128)(2,1)S(1)}, bf16[1,16,64,512]{3,1,2,0:T(8,128)(2,1)}, bf16[1,16,64,512]{3,1,2,0:T(8,128)(2,1)}) fusion(f32[16,64,512]{2,0,1:T(8,128)S(1)} %copy-done.2, f32[16,64,512]{2,0,1:T(8,128)} %fusion.77, f32[16,64]{0,1:T(8,128)S(1)} %get-tuple-element.23, ...), kind=kOutput, calls=%fused_computation.58 | convolution fusion | flops 59770624 | bytes 11542528 | tf_op jit(solution)/shard_map/an,njw->ajw/dot_general | solution.py:44
  142.4 0.2 pad_maximum_fusion.2
  142.6 2.5 copy.59
  145.2 4.3 %all-to-all-start.3 = ((bf16[2,16,64,512]{3,2,0,1:T(8,128)(2,1)}), bf16[2,16,64,512]{3,2,0,1:T(8,128)(2,1)}, u32[]{:S(2)}, u32[]{:S(2)}) async-start(bf16[2,16,64,512]{3,2,0,1:T(8,128)(2,1)} %copy.59), calls=%async_computation.3 | async-start | bytes 4194304 | tf_op jit(solution)/shard_map/all_to_all | solution.py:113
  149.5 1.7 pad_maximum_fusion.1
  151.3 2.5 copy.51
  153.7 22.4 %all-to-all-done.3 = bf16[2,16,64,512]{3,2,0,1:T(8,128)(2,1)} async-done(((bf16[2,16,64,512]{3,2,0,1:T(8,128)(2,1)}), bf16[2,16,64,512]{3,2,0,1:T(8,128)(2,1)}, u32[]{:S(2)}, u32[]{:S(2)}) %all-to-all-start.3) | async-done | bytes 2097184 | tf_op jit(solution)/shard_map/all_to_all | solution.py:113
  176.2 4.5 %all-to-all-start.1 = ((bf16[2,16,64,512]{3,2,0,1:T(8,128)(2,1)}), bf16[2,16,64,512]{3,2,0,1:T(8,128)(2,1)}, u32[]{:S(2)}, u32[]{:S(2)}) async-start(bf16[2,16,64,512]{3,2,0,1:T(8,128)(2,1)} %copy.51), calls=%async_computation.1 | async-start | bytes 4194304 | tf_op jit(solution)/shard_map/all_to_all | solution.py:122
  180.7 1.8 copy.60
  182.5 0.2 fusion.198
  182.7 0.1 copy.63
  182.8 0.1 copy.61
  182.9 6.9 %fusion.64 = f32[2,512,512]{2,1,0:T(8,128)S(1)} fusion(bf16[2,512,512]{2,1,0:T(8,128)(2,1)S(1)} %bitcast.141), kind=kOutput, calls=%fused_computation.78 | convolution fusion | flops 3224895488 | bytes 3145728 | tf_op jit(solution)/shard_map/bj,ejw->ebw/dot_general | solution.py:49
  189.8 6.9 %fusion.60 = f32[2,512,512]{2,1,0:T(8,128)S(1)} fusion(bf16[2,512,512]{2,1,0:T(8,128)(2,1)S(1)} %bitcast.139), kind=kOutput, calls=%fused_computation.74 | convolution fusion | flops 3224895488 | bytes 3145728 | tf_op jit(solution)/shard_map/bj,ejw->ebw/dot_general | solution.py:52
  196.8 7.4 %convolution_add_fusion = f32[2,512,512]{2,1,0:T(8,128)} fusion(f32[2,512,512]{2,1,0:T(8,128)S(1)} %fusion.64, bf16[2,512,512]{2,1,0:T(8,128)(2,1)S(1)} %bitcast.140), kind=kOutput, calls=%fused_computation.44 | convolution fusion | flops 3225419776 | bytes 5242880 | tf_op jit(solution)/shard_map/bj,ejw->ebw/dot_general | solution.py:49
  204.2 7.6 %convolution_subtract_fusion = f32[2,512,512]{2,1,0:T(8,128)} fusion(f32[2,512,512]{2,1,0:T(8,128)S(1)} %fusion.60, bf16[2,512,512]{2,1,0:T(8,128)(2,1)S(1)} %bitcast.142), kind=kOutput, calls=%fused_computation.42 | convolution fusion | flops 3225419776 | bytes 5242880 | tf_op jit(solution)/shard_map/bj,ejw->ebw/dot_general | solution.py:52
  211.8 0.0 all-to-all-done.1
  211.8 1.8 copy.52
  213.6 0.2 fusion.199
  213.8 0.1 copy.53
  213.9 0.1 copy.55
  214.0 6.9 %fusion.62 = f32[2,512,512]{2,1,0:T(8,128)S(1)} fusion(bf16[2,512,512]{2,1,0:T(8,128)(2,1)S(1)} %bitcast.143), kind=kOutput, calls=%fused_computation.76 | convolution fusion | flops 3224895488 | bytes 3145728 | tf_op jit(solution)/shard_map/bj,ejw->ebw/dot_general | solution.py:52
  220.9 6.9 %fusion.66 = f32[2,512,512]{2,1,0:T(8,128)S(1)} fusion(bf16[2,512,512]{2,1,0:T(8,128)(2,1)S(1)} %bitcast.136), kind=kOutput, calls=%fused_computation.80 | convolution fusion | flops 3224895488 | bytes 3145728 | tf_op jit(solution)/shard_map/bj,ejw->ebw/dot_general | solution.py:49
  227.9 7.4 %convolution_add_fusion.1 = f32[2,512,512]{2,1,0:T(8,128)S(1)} fusion(f32[2,512,512]{2,1,0:T(8,128)S(1)} %fusion.66, bf16[2,512,512]{2,1,0:T(8,128)(2,1)S(1)} %bitcast.144), kind=kOutput, calls=%fused_computation.45 | convolution fusion | flops 3225419776 | bytes 5242880 | tf_op jit(solution)/shard_map/bj,ejw->ebw/dot_general | solution.py:49
  235.3 7.5 %multiply_subtract_fusion = (f32[2,512,512]{2,1,0:T(8,128)S(1)}, f32[2,512,512]{2,1,0:T(8,128)S(1)}) fusion(f32[2,512,512]{2,1,0:T(8,128)S(1)} %copy-done.5, f32[2,512,512]{2,1,0:T(8,128)S(1)} %convolution_add_fusion.1, f32[2,512,512]{2,1,0:T(8,128)S(1)} %copy-done.4, f32[2,512,512]{2,1,0:T(8,128)S(1)} %fusion.62, bf16[2,512,512]{2,1,0:T(8,128)(2,1)S(1)} %bitcast.137), kind=kOutput, calls=%fused_computation.36 | convolution fusion | flops 3228565504 | bytes 13631488 | tf_op jit(solution)/shard_map/bj,ejw->ebw/dot_general | solution.py:52
  242.8 8.4 %fusion.10 = f32[2,512,512]{2,1,0:T(8,128)S(1)} fusion(f32[2,512,512]{2,1,0:T(8,128)S(1)} %get-tuple-element.6), kind=kOutput, calls=%fused_computation.17 | convolution fusion | flops 3224895488 | bytes 4194304 | tf_op jit(solution)/shard_map/jb,ebw->ejw/dot_general | solution.py:65
  251.2 8.6 %fusion.12 = f32[2,512,512]{2,1,0:T(8,128)S(1)} fusion(f32[2,512,512]{2,1,0:T(8,128)S(1)} %get-tuple-element.6), kind=kOutput, calls=%fused_computation.19 | convolution fusion | flops 3224895488 | bytes 4194304 | tf_op jit(solution)/shard_map/jb,ebw->ejw/dot_general | solution.py:62
  259.8 8.5 %subtract_bitcast_fusion = f32[1,2,512,512]{2,3,1,0:T(8,128)S(1)} fusion(f32[2,512,512]{2,1,0:T(8,128)S(1)} %fusion.12, f32[2,512,512]{2,1,0:T(8,128)S(1)} %get-tuple-element.5), kind=kOutput, calls=%fused_computation.34 | convolution fusion | flops 3225419776 | bytes 6291456 | tf_op jit(solution)/shard_map/jb,ebw->ejw/dot_general | solution.py:62
  268.3 8.5 %add_bitcast_fusion = f32[1,2,512,512]{2,3,1,0:T(8,128)S(1)} fusion(f32[2,512,512]{2,1,0:T(8,128)S(1)} %fusion.10, f32[2,512,512]{2,1,0:T(8,128)S(1)} %get-tuple-element.5), kind=kOutput, calls=%fused_computation.33 | convolution fusion | flops 3225419776 | bytes 6291456 | tf_op jit(solution)/shard_map/jb,ebw->ejw/dot_general | solution.py:65
  276.7 2.4 pad_maximum_fusion
  279.1 7.3 %copy.69 = f32[2,2,512,512]{3,1,0,2:T(2,128)} copy(f32[2,2,512,512]{2,3,1,0:T(8,128)} %pad_maximum_fusion) | data formatting | bytes 8388608 | tf_op jit(solution)/shard_map/stack | solution.py:69
  286.4 53.4 %all_to_all.69 = f32[2,2,512,512]{3,1,0,2:T(2,128)S(1)} all-to-all(f32[2,2,512,512]{3,1,0,2:T(2,128)} %copy.69), channel_id=1, replica_groups=mesh['ctx'=8,'tp'=4] {'ctx'}, dimensions={2} | all-to-all | bytes 8388608 | tf_op jit(solution)/shard_map/all_to_all | solution.py:68
  339.8 1.3 copy.70
  341.2 2.0 fusion.197
  343.1 3.0 copy.71
  346.1 3.6 squeeze.34
  349.8 4.6 %copy.72 = f32[1,8,2,64,512]{4,2,1,3,0:T(2,128)} copy(f32[1,8,2,64,512]{4,3,1,2,0:T(8,128)} %get-tuple-element.12) | data formatting | bytes 4194304 | tf_op jit(solution)/shard_map/slice | solution.py:71
  354.3 3.6 squeeze.35
  358.0 3.7 fusion.18
  361.7 1.4 fusion.39
  363.2 0.0 copy-start.7
  363.2 0.6 copy.73
  363.8 17.8 %all_to_all.70 = f32[8,64,512]{2,1,0:T(8,128)S(1)} all-to-all(f32[8,64,512]{2,1,0:T(8,128)S(1)} %copy.73), channel_id=1, replica_groups=mesh['ctx'=8,'tp'=4] {'ctx'}, dimensions={0} | all-to-all | bytes 2097152 | tf_op jit(solution)/shard_map/all_to_all | solution.py:78
  381.6 1.3 fusion.50
  (21 shorter events, 0.1 us)
Async XLA Ops:
  6.5 5.9 %copy-start.6 = (f32[3,3,512]{2,1,0:T(4,128)S(1)}, f32[3,3,512]{2,1,0:T(4,128)}, u32[]{:S(2)}) copy-start(f32[3,3,512]{2,1,0:T(4,128)} %param.9) | copy-start | bytes 55300
  6.5 85.9 %all-gather.2.cloned.1.call-start = ((), (), s32[]{:S(2)}) async-start(), calls=%async_computation.6 | async-start | bytes 5242880 | tf_op jit(solution)/shard_map/all_gather | solution.py:84
  7.3 103.7 %all-to-all-start.2 = ((f32[8,64,512]{2,1,0:T(8,128)}), f32[8,64,512]{2,1,0:T(8,128)}, u32[]{:S(2)}, u32[]{:S(2)}) async-start(f32[8,64,512]{2,1,0:T(8,128)} %bitcast.138), calls=%async_computation.2 | async-start | bytes 2097152 | tf_op jit(solution)/shard_map/all_to_all | solution.py:112
  12.4 83.2 %copy-start.8 = (f32[4096]{0:T(1024)S(1)}, f32[4096]{0:T(1024)}, u32[]{:S(2)}) copy-start(f32[4096]{0:T(1024)} %param.7) | copy-start | bytes 49156
  92.4 3.4 copy-start.3
  105.8 2.6 collective-permute-start
  110.9 22.0 %all-to-all-start = ((f32[8,64,512]{2,1,0:T(8,128)}), f32[8,64,512]{2,1,0:T(8,128)}, u32[]{:S(2)}, u32[]{:S(2)}) async-start(f32[8,64,512]{2,1,0:T(8,128)} %bitcast.135), calls=%async_computation | async-start | bytes 2097152 | tf_op jit(solution)/shard_map/all_to_all | solution.py:121
  132.9 3.6 copy-start.2
  145.2 31.0 %all-to-all-start.3 = ((bf16[2,16,64,512]{3,2,0,1:T(8,128)(2,1)}), bf16[2,16,64,512]{3,2,0,1:T(8,128)(2,1)}, u32[]{:S(2)}, u32[]{:S(2)}) async-start(bf16[2,16,64,512]{3,2,0,1:T(8,128)(2,1)} %copy.59), calls=%async_computation.3 | async-start | bytes 4194304 | tf_op jit(solution)/shard_map/all_to_all | solution.py:113
  176.2 35.6 %all-to-all-start.1 = ((bf16[2,16,64,512]{3,2,0,1:T(8,128)(2,1)}), bf16[2,16,64,512]{3,2,0,1:T(8,128)(2,1)}, u32[]{:S(2)}, u32[]{:S(2)}) async-start(bf16[2,16,64,512]{3,2,0,1:T(8,128)(2,1)} %copy.51), calls=%async_computation.1 | async-start | bytes 4194304 | tf_op jit(solution)/shard_map/all_to_all | solution.py:122
  227.8 7.4 %copy-start.4 = (f32[2,512,512]{2,1,0:T(8,128)S(1)}, f32[2,512,512]{2,1,0:T(8,128)}, u32[]{:S(2)}) copy-start(f32[2,512,512]{2,1,0:T(8,128)} %convolution_add_fusion) | copy-start | bytes 6291460
  227.8 7.4 %copy-start.5 = (f32[2,512,512]{2,1,0:T(8,128)S(1)}, f32[2,512,512]{2,1,0:T(8,128)}, u32[]{:S(2)}) copy-start(f32[2,512,512]{2,1,0:T(8,128)} %convolution_subtract_fusion) | copy-start | bytes 6291460
  358.0 3.8 copy-start
  358.0 3.8 copy-start.1
  363.2 18.4 %copy-start.7 = (f32[512]{0:T(512)S(1)}, f32[512]{0:T(512)}, u32[]{:S(2)}) copy-start(f32[512]{0:T(512)} %param.11) | copy-start | bytes 6148
Sparse Core Ops, SparseCore 0:
  8.9 83.4 all-gather.1
where the time goes:
time: 395 us; the launch traced here: 390 us
  matrix products  126 us (32%)
  waiting for transfers between devices  110 us (28%)
  blocking collectives  71.2 us (18%)
  local copies, waits for them, and re-layouts  35.7 us (9%)
  starting transfers between devices  22.4 us (6%)
  between operations  14 us (4%)
  other arithmetic  11.6 us (3%)
    all_gather x1, waiting for transfers between devices, body(): gathered = lax.all_gather(tokens, 'tp', axis=1, tiled=True)  79.9 us
    all_to_all x1, blocking collectives, inverse_transform(): lax.all_to_all(jnp.stack([back_real, back_imag]), 'ctx', split_axis=2, co...  53.4 us
    all_to_all x2, waiting for transfers between devices, body(): lax.all_to_all(values.astype(jnp.bfloat16), 'ctx', split_axis=1, concat_a...  22.4 us
    all_to_all x1, blocking collectives, inverse_transform(): lax.all_to_all(folded.reshape(row_count, width_all), 'ctx', split_axis=0,...  17.8 us
    dot_general x2, matrix products, forward_transform(): jnp.einsum('bj,ejw->ebw', inner_sin, arrived[0], precision=highest)  15.1 us
    dot_general x2, matrix products, forward_transform(): jnp.einsum('bj,ejw->ebw', inner_sin, arrived[1], precision=highest)  14.8 us
    dot_general x2, matrix products, forward_transform(): jnp.einsum('bj,ejw->ebw', inner_cos, arrived[0], precision=highest)  13.8 us
    dot_general x2, matrix products, forward_transform(): jnp.einsum('bj,ejw->ebw', inner_cos, arrived[1], precision=highest)  13.8 us
  transfers between devices with their start and end apart: 6, of which 4 were waited for; matrix products, arithmetic and copies ran while one was open for 16% of the time, Pallas kernels for 0%

commit v1 on v0

--- a/solution.py
+++ b/solution.py
@@ -81,7 +81,12 @@
 
 
 def body(tokens, norm_gain, proj_weight, short_taps, long_filter, skip_gain):
-    gathered = lax.all_gather(tokens, "tp", axis=1, tiled=True)
+    ring = [tokens]
+    for hop in range(3):
+        ring.append(lax.ppermute(ring[-1], "tp", [(dev, (dev + 1) % 4) for dev in range(4)]))
+    gathered = jnp.roll(
+        jnp.concatenate(ring[::-1], axis=1), (lax.axis_index("tp") + 1) * ring[0].shape[1], axis=1
+    )
     widened = gathered.astype(jnp.float32)
     scaling = lax.rsqrt(jnp.mean(widened * widened, axis=1, keepdims=True) + 1e-06)
     normed = (widened * scaling * norm_gain).astype(jnp.bfloat16)

time: 395 us -> 379 us (0.959)
  between operations: 14 us -> 0.74 us
  waiting for transfers between devices: 110 us -> 104 us
  local copies, waits for them, and re-layouts: 35.7 us -> 40.4 us
  matrix products: 126 us -> 122 us
    all_gather x1 -> x0, waiting for transfers between devices: 79.9 us -> none  [body(): gathered = lax.all_gather(tokens, 'tp', axis=1, tiled=True)]
    ppermute x0 -> x3, waiting for transfers between devices: none -> 72.4 us  [body(): lax.ppermute(ring[-1], 'tp', [(dev, (dev + 1) % 4) for dev in range(4)])]
    unnamed x20 -> x33, local copies, waits for them, and re-layouts: 0.25 us -> 4.96 us
  transfers between devices with their start and end apart: 6 -> 8, of which waited for: 4 -> 7; matrix products, arithmetic and copies ran while one was open for 16% -> 13% of each run, Pallas kernels for 0% -> 0%
where the time goes in v1:
time: 379 us; the launch traced here: 372 us
  matrix products  122 us (32%)
  waiting for transfers between devices  104 us (27%)
  blocking collectives  70.7 us (19%)
  local copies, waits for them, and re-layouts  40.4 us (11%)
  starting transfers between devices  24 us (6%)
  other arithmetic  9.33 us (2%)
    ppermute x3, waiting for transfers between devices, body(): lax.ppermute(ring[-1], 'tp', [(dev, (dev + 1) % 4) for dev in range(4)])  72.4 us
    all_to_all x1, blocking collectives, inverse_transform(): lax.all_to_all(jnp.stack([back_real, back_imag]), 'ctx', split_axis=2, co...  52.9 us
    all_to_all x2, waiting for transfers between devices, body(): lax.all_to_all(values.astype(jnp.bfloat16), 'ctx', split_axis=1, concat_a...  25.1 us
    all_to_all x1, blocking collectives, inverse_transform(): lax.all_to_all(folded.reshape(row_count, width_all), 'ctx', split_axis=0,...  17.8 us
    dot_general x2, matrix products, forward_transform(): jnp.einsum('bj,ejw->ebw', inner_sin, arrived[0], precision=highest)  14.9 us
    dot_general x2, matrix products, forward_transform(): jnp.einsum('bj,ejw->ebw', inner_cos, arrived[0], precision=highest)  14.5 us
    dot_general x2, matrix products, forward_transform(): jnp.einsum('bj,ejw->ebw', inner_sin, arrived[1], precision=highest)  14.4 us
    dot_general x2, matrix products, forward_transform(): jnp.einsum('bj,ejw->ebw', inner_cos, arrived[1], precision=highest)  13.8 us
  transfers between devices with their start and end apart: 8, of which 7 were waited for; matrix products, arithmetic and copies ran while one was open for 13% of the time, Pallas kernels for 0%

profile of v1, /device:TPU:0, one launch (start us, length us, event | category | flops | bytes accessed | tf_op | source)
XLA Modules:
  0.0 371.7 jit_solution(7892730234983237749)
XLA Ops:
  0.0 3.0 collective-permute-start
  3.0 25.4 %collective-permute-done = bf16[512,1024]{1,0:T(8,128)(2,1)S(1)} collective-permute-done((bf16[512,1024]{1,0:T(8,128)(2,1)}, bf16[512,1024]{1,0:T(8,128)(2,1)S(1)}, u32[]{:S(2)}, u32[]{:S(2)}) %collective-permute-start) | collective-permute-done | bytes 1048608 | tf_op jit(solution)/shard_map/ppermute | solution.py:86
  28.4 26.1 %collective-permute-done.1 = bf16[512,1024]{1,0:T(8,128)(2,1)S(1)} collective-permute-done((bf16[512,1024]{1,0:T(8,128)(2,1)S(1)}, bf16[512,1024]{1,0:T(8,128)(2,1)S(1)}, u32[]{:S(2)}, u32[]{:S(2)}) %collective-permute-start.1) | collective-permute-done | bytes 1048608 | tf_op jit(solution)/shard_map/ppermute | solution.py:86
  54.6 4.2 %all-to-all-start.2 = ((f32[8,64,512]{2,1,0:T(8,128)}), f32[8,64,512]{2,1,0:T(8,128)}, u32[]{:S(2)}, u32[]{:S(2)}) async-start(f32[8,64,512]{2,1,0:T(8,128)} %bitcast.138), calls=%async_computation.2 | async-start | bytes 2097152 | tf_op jit(solution)/shard_map/all_to_all | solution.py:117
  58.9 20.9 %collective-permute-done.2 = bf16[512,1024]{1,0:T(8,128)(2,1)S(1)} collective-permute-done((bf16[512,1024]{1,0:T(8,128)(2,1)S(1)}, bf16[512,1024]{1,0:T(8,128)(2,1)S(1)}, u32[]{:S(2)}, u32[]{:S(2)}) %collective-permute-start.2) | collective-permute-done | bytes 1048608 | tf_op jit(solution)/shard_map/ppermute | solution.py:86
  80.0 0.1 constant_dynamic-update-slice_fusion.5
  80.1 1.0 copy-done.3
  81.4 0.1 constant_dynamic-update-slice_fusion.1
  81.6 0.9 fusion
  82.5 3.3 copy-done.9
  85.8 6.7 %fusion.34 = bf16[3,512,512]{2,1,0:T(8,128)(2,1)S(1)} fusion(bf16[3,4096,512]{2,1,0:T(8,128)(2,1)S(1)} %copy-done.9, f32[4096]{0:T(1024)S(1)} %copy-done.10, f32[512]{0:T(512)S(1)} %add_rsqrt_fusion, bf16[512,8192]{1,0:T(8,128)(2,1)S(1)} %constant_dynamic-update-slice_fusion, s32[]{:T(128)S(6)} %select_n.71), kind=kOutput, calls=%fused_computation.51 | convolution fusion | flops 6451625984 | bytes 18368516 | tf_op jit(solution)/shard_map/td,bdc->btc/dot_general | solution.py:93
  92.5 1.3 collective-permute-start.3
  93.9 0.8 collective-permute-done.3
  94.6 0.5 maximum_convert_fusion
  95.1 0.9 fusion.9
  96.1 1.2 slice_multiply_fusion.3
  97.2 6.6 %all-to-all-start = ((f32[8,64,512]{2,1,0:T(8,128)}), f32[8,64,512]{2,1,0:T(8,128)}, u32[]{:S(2)}, u32[]{:S(2)}) async-start(f32[8,64,512]{2,1,0:T(8,128)} %bitcast.135), calls=%async_computation | async-start | bytes 2097152 | tf_op jit(solution)/shard_map/all_to_all | solution.py:126
  103.8 0.2 fusion.105
  104.1 4.7 %fusion.76 = f32[16,64,512]{2,0,1:T(8,128)} fusion(f32[8,64,512]{2,1,0:T(8,128)} %all-to-all-done.2), kind=kOutput, calls=%fused_computation.90 | convolution fusion | flops 50333440 | bytes 3145728 | tf_op jit(solution)/shard_map/an,njw->ajw/dot_general | solution.py:45
  108.8 4.8 %fusion.78 = f32[16,64,512]{2,0,1:T(8,128)} fusion(f32[8,64,512]{2,1,0:T(8,128)} %all-to-all-done.2), kind=kOutput, calls=%fused_computation.92 | convolution fusion | flops 50333440 | bytes 3145728 | tf_op jit(solution)/shard_map/an,njw->ajw/dot_general | solution.py:44
  113.6 5.7 %all-to-all-done = f32[8,64,512]{2,1,0:T(8,128)} async-done(((f32[8,64,512]{2,1,0:T(8,128)}), f32[8,64,512]{2,1,0:T(8,128)}, u32[]{:S(2)}, u32[]{:S(2)}) %all-to-all-start) | async-done | bytes 1048608 | tf_op jit(solution)/shard_map/all_to_all | solution.py:126
  119.3 3.6 fusion.80
  122.9 5.9 %fusion.48 = (bf16[1,16,64,512]{3,1,2,0:T(8,128)(2,1)S(1)}, bf16[1,16,64,512]{3,1,2,0:T(8,128)(2,1)S(1)}, bf16[1,16,64,512]{3,1,2,0:T(8,128)(2,1)}, bf16[1,16,64,512]{3,1,2,0:T(8,128)(2,1)}) fusion(f32[16,64,512]{2,0,1:T(8,128)S(1)} %copy-done.2, f32[16,64,512]{2,0,1:T(8,128)} %fusion.78, f32[16,64]{0,1:T(8,128)S(1)} %get-tuple-element.23, ...), kind=kOutput, calls=%fused_computation.59 | convolution fusion | flops 59770624 | bytes 11542528 | tf_op jit(solution)/shard_map/an,njw->ajw/dot_general | solution.py:44
  128.8 0.2 pad_maximum_fusion.2
  129.0 2.5 copy.59
  131.5 4.3 %all-to-all-start.3 = ((bf16[2,16,64,512]{3,2,0,1:T(8,128)(2,1)}), bf16[2,16,64,512]{3,2,0,1:T(8,128)(2,1)}, u32[]{:S(2)}, u32[]{:S(2)}) async-start(bf16[2,16,64,512]{3,2,0,1:T(8,128)(2,1)} %copy.59), calls=%async_computation.3 | async-start | bytes 4194304 | tf_op jit(solution)/shard_map/all_to_all | solution.py:118
  135.9 1.7 pad_maximum_fusion.1
  137.6 2.5 copy.51
  140.1 22.4 %all-to-all-done.3 = bf16[2,16,64,512]{3,2,0,1:T(8,128)(2,1)} async-done(((bf16[2,16,64,512]{3,2,0,1:T(8,128)(2,1)}), bf16[2,16,64,512]{3,2,0,1:T(8,128)(2,1)}, u32[]{:S(2)}, u32[]{:S(2)}) %all-to-all-start.3) | async-done | bytes 2097184 | tf_op jit(solution)/shard_map/all_to_all | solution.py:118
  162.5 4.5 %all-to-all-start.1 = ((bf16[2,16,64,512]{3,2,0,1:T(8,128)(2,1)}), bf16[2,16,64,512]{3,2,0,1:T(8,128)(2,1)}, u32[]{:S(2)}, u32[]{:S(2)}) async-start(bf16[2,16,64,512]{3,2,0,1:T(8,128)(2,1)} %copy.51), calls=%async_computation.1 | async-start | bytes 4194304 | tf_op jit(solution)/shard_map/all_to_all | solution.py:127
  167.0 1.8 copy.60
  168.8 0.2 fusion.200
  169.0 0.1 copy.63
  169.2 6.9 %fusion.61 = f32[2,512,512]{2,1,0:T(8,128)S(1)} fusion(bf16[2,512,512]{2,1,0:T(8,128)(2,1)S(1)} %bitcast.139), kind=kOutput, calls=%fused_computation.75 | convolution fusion | flops 3224895488 | bytes 3145728 | tf_op jit(solution)/shard_map/bj,ejw->ebw/dot_general | solution.py:52
  176.2 7.4 %fusion.65 = f32[2,512,512]{2,1,0:T(8,128)} fusion(bf16[2,512,512]{2,1,0:T(8,128)(2,1)S(1)} %bitcast.141), kind=kOutput, calls=%fused_computation.79 | convolution fusion | flops 3224895488 | bytes 3145728 | tf_op jit(solution)/shard_map/bj,ejw->ebw/dot_general | solution.py:49
  183.5 7.4 %convolution_subtract_fusion = f32[2,512,512]{2,1,0:T(8,128)} fusion(f32[2,512,512]{2,1,0:T(8,128)S(1)} %fusion.61, bf16[2,512,512]{2,1,0:T(8,128)(2,1)S(1)} %bitcast.142), kind=kOutput, calls=%fused_computation.43 | convolution fusion | flops 3225419776 | bytes 5242880 | tf_op jit(solution)/shard_map/bj,ejw->ebw/dot_general | solution.py:52
  191.0 2.7 all-to-all-done.1
  193.7 1.8 copy.52
  195.5 0.2 fusion.201
  195.7 0.1 copy.53
  195.8 7.1 %fusion.67 = f32[2,512,512]{2,1,0:T(8,128)S(1)} fusion(bf16[2,512,512]{2,1,0:T(8,128)(2,1)S(1)} %bitcast.136), kind=kOutput, calls=%fused_computation.81 | convolution fusion | flops 3224895488 | bytes 3145728 | tf_op jit(solution)/shard_map/bj,ejw->ebw/dot_general | solution.py:49
  202.9 0.1 copy.55
  203.0 6.9 %fusion.63 = f32[2,512,512]{2,1,0:T(8,128)S(1)} fusion(bf16[2,512,512]{2,1,0:T(8,128)(2,1)S(1)} %bitcast.143), kind=kOutput, calls=%fused_computation.77 | convolution fusion | flops 3224895488 | bytes 3145728 | tf_op jit(solution)/shard_map/bj,ejw->ebw/dot_general | solution.py:52
  209.9 7.0 %convolution_add_fusion.1 = f32[2,512,512]{2,1,0:T(8,128)S(1)} fusion(f32[2,512,512]{2,1,0:T(8,128)S(1)} %fusion.67, bf16[2,512,512]{2,1,0:T(8,128)(2,1)S(1)} %bitcast.144), kind=kOutput, calls=%fused_computation.46 | convolution fusion | flops 3225419776 | bytes 5242880 | tf_op jit(solution)/shard_map/bj,ejw->ebw/dot_general | solution.py:49
  216.9 7.4 %convolution_add_fusion = f32[2,512,512]{2,1,0:T(8,128)S(1)} fusion(f32[2,512,512]{2,1,0:T(8,128)S(1)} %copy-done.11, bf16[2,512,512]{2,1,0:T(8,128)(2,1)S(1)} %bitcast.140), kind=kOutput, calls=%fused_computation.45 | convolution fusion | flops 3225419776 | bytes 5242880 | tf_op jit(solution)/shard_map/bj,ejw->ebw/dot_general | solution.py:49
  224.4 7.5 %multiply_subtract_fusion = (f32[2,512,512]{2,1,0:T(8,128)S(1)}, f32[2,512,512]{2,1,0:T(8,128)S(1)}) fusion(f32[2,512,512]{2,1,0:T(8,128)S(1)} %copy-done.4, f32[2,512,512]{2,1,0:T(8,128)S(1)} %convolution_add_fusion.1, f32[2,512,512]{2,1,0:T(8,128)S(1)} %convolution_add_fusion, f32[2,512,512]{2,1,0:T(8,128)S(1)} %fusion.63, ...), kind=kOutput, calls=%fused_computation.37 | convolution fusion | flops 3228565504 | bytes 13631488 | tf_op jit(solution)/shard_map/bj,ejw->ebw/dot_general | solution.py:52
  231.9 8.4 %fusion.11 = f32[2,512,512]{2,1,0:T(8,128)S(1)} fusion(f32[2,512,512]{2,1,0:T(8,128)S(1)} %get-tuple-element.6), kind=kOutput, calls=%fused_computation.18 | convolution fusion | flops 3224895488 | bytes 4194304 | tf_op jit(solution)/shard_map/jb,ebw->ejw/dot_general | solution.py:65
  240.3 8.6 %fusion.13 = f32[2,512,512]{2,1,0:T(8,128)S(1)} fusion(f32[2,512,512]{2,1,0:T(8,128)S(1)} %get-tuple-element.6), kind=kOutput, calls=%fused_computation.20 | convolution fusion | flops 3224895488 | bytes 4194304 | tf_op jit(solution)/shard_map/jb,ebw->ejw/dot_general | solution.py:62
  248.9 8.5 %add_bitcast_fusion = f32[1,2,512,512]{2,3,1,0:T(8,128)S(1)} fusion(f32[2,512,512]{2,1,0:T(8,128)S(1)} %fusion.11, f32[2,512,512]{2,1,0:T(8,128)S(1)} %get-tuple-element.5), kind=kOutput, calls=%fused_computation.34 | convolution fusion | flops 3225419776 | bytes 6291456 | tf_op jit(solution)/shard_map/jb,ebw->ejw/dot_general | solution.py:65
  257.4 8.5 %subtract_bitcast_fusion = f32[1,2,512,512]{2,3,1,0:T(8,128)S(1)} fusion(f32[2,512,512]{2,1,0:T(8,128)S(1)} %fusion.13, f32[2,512,512]{2,1,0:T(8,128)S(1)} %get-tuple-element.5), kind=kOutput, calls=%fused_computation.35 | convolution fusion | flops 3225419776 | bytes 6291456 | tf_op jit(solution)/shard_map/jb,ebw->ejw/dot_general | solution.py:62
  265.8 2.4 pad_maximum_fusion
  268.2 7.3 %copy.69 = f32[2,2,512,512]{3,1,0,2:T(2,128)} copy(f32[2,2,512,512]{2,3,1,0:T(8,128)} %pad_maximum_fusion) | data formatting | bytes 8388608 | tf_op jit(solution)/shard_map/stack | solution.py:69
  275.5 52.9 %all_to_all.69 = f32[2,2,512,512]{3,1,0,2:T(2,128)S(1)} all-to-all(f32[2,2,512,512]{3,1,0,2:T(2,128)} %copy.69), channel_id=1, replica_groups=mesh['ctx'=8,'tp'=4] {'ctx'}, dimensions={2} | all-to-all | bytes 8388608 | tf_op jit(solution)/shard_map/all_to_all | solution.py:68
  328.4 1.3 copy.70
  329.8 1.9 fusion.199
  331.7 3.0 copy.72
  334.7 3.6 squeeze.35
  338.3 4.6 %copy.71 = f32[1,8,2,64,512]{4,2,1,3,0:T(2,128)} copy(f32[1,8,2,64,512]{4,3,1,2,0:T(8,128)} %get-tuple-element.11) | data formatting | bytes 4194304 | tf_op jit(solution)/shard_map/slice | solution.py:71
  342.9 3.6 squeeze.34
  346.5 3.7 %fusion.19 = f32[8,64,512]{2,0,1:T(8,128)S(1)} fusion(f32[16,64,512]{2,0,1:T(8,128)} %squeeze.35, f32[16,64,512]{2,0,1:T(8,128)} %squeeze.34, f32[16,64]{0,1:T(8,128)S(1)} %get-tuple-element.23, f32[16,64]{0,1:T(8,128)S(1)} %get-tuple-element.22), kind=kOutput, calls=%fused_computation.26 | convolution fusion | flops 51906304 | bytes 5251072 | tf_op jit(solution)/shard_map/an,ajw->njw/dot_general | solution.py:76
  350.3 1.4 fusion.40
  351.7 0.6 copy.73
  352.4 17.8 %all_to_all.70 = f32[8,64,512]{2,1,0:T(8,128)S(1)} all-to-all(f32[8,64,512]{2,1,0:T(8,128)S(1)} %copy.73), channel_id=1, replica_groups=mesh['ctx'=8,'tp'=4] {'ctx'}, dimensions={0} | all-to-all | bytes 2097152 | tf_op jit(solution)/shard_map/all_to_all | solution.py:78
  370.2 1.3 fusion.51
  (38 shorter events, 0.7 us)
Async XLA Ops:
  0.0 58.8 %copy-start.7 = (f32[3,3,512]{2,1,0:T(4,128)S(1)}, f32[3,3,512]{2,1,0:T(4,128)}, u32[]{:S(2)}) copy-start(f32[3,3,512]{2,1,0:T(4,128)} %param.9) | copy-start | bytes 55300
  0.0 28.4 %collective-permute-start = (bf16[512,1024]{1,0:T(8,128)(2,1)}, bf16[512,1024]{1,0:T(8,128)(2,1)S(1)}, u32[]{:S(2)}, u32[]{:S(2)}) collective-permute-start(bf16[512,1024]{1,0:T(8,128)(2,1)} %param.6), channel_id=1, source_target_pairs={{0,1},{1,2},{2,3},{3,0},{4,5},{5,6},{6,7},{7,4},{8,9},{9,10},{10,1... | collective-permute-start | bytes 3145736 | tf_op jit(solution)/shard_map/ppermute | solution.py:86
  28.4 26.1 %collective-permute-start.1 = (bf16[512,1024]{1,0:T(8,128)(2,1)S(1)}, bf16[512,1024]{1,0:T(8,128)(2,1)S(1)}, u32[]{:S(2)}, u32[]{:S(2)}) collective-permute-start(bf16[512,1024]{1,0:T(8,128)(2,1)S(1)} %collective-permute-done), channel_id=1, source_target_pairs={{0,1},{1,2},{2,3},{3,0},{4,5},{5,6},{6,7},{7,4},{8,9},{9,10},{10,1... | collective-permute-start | bytes 3145736 | tf_op jit(solution)/shard_map/ppermute | solution.py:86
  54.6 25.2 %collective-permute-start.2 = (bf16[512,1024]{1,0:T(8,128)(2,1)S(1)}, bf16[512,1024]{1,0:T(8,128)(2,1)S(1)}, u32[]{:S(2)}, u32[]{:S(2)}) collective-permute-start(bf16[512,1024]{1,0:T(8,128)(2,1)S(1)} %collective-permute-done.1), channel_id=1, source_target_pairs={{0,1},{1,2},{2,3},{3,0},{4,5},{5,6},{6,7},{7,4},{8,9},{9,10},{10,1... | collective-permute-start | bytes 3145736 | tf_op jit(solution)/shard_map/ppermute | solution.py:86
  54.6 42.7 %all-to-all-start.2 = ((f32[8,64,512]{2,1,0:T(8,128)}), f32[8,64,512]{2,1,0:T(8,128)}, u32[]{:S(2)}, u32[]{:S(2)}) async-start(f32[8,64,512]{2,1,0:T(8,128)} %bitcast.138), calls=%async_computation.2 | async-start | bytes 2097152 | tf_op jit(solution)/shard_map/all_to_all | solution.py:117
  79.9 1.2 copy-start.3
  81.1 1.4 copy-start.10
  81.2 4.6 %copy-start.9 = (bf16[3,4096,512]{2,1,0:T(8,128)(2,1)S(1)}, bf16[3,4096,512]{2,1,0:T(8,128)(2,1)}, u32[]{:S(2)}) copy-start(bf16[3,4096,512]{2,1,0:T(8,128)(2,1)} %param.8) | copy-start | bytes 37748740
  92.5 2.1 collective-permute-start.3
  97.2 22.1 %all-to-all-start = ((f32[8,64,512]{2,1,0:T(8,128)}), f32[8,64,512]{2,1,0:T(8,128)}, u32[]{:S(2)}, u32[]{:S(2)}) async-start(f32[8,64,512]{2,1,0:T(8,128)} %bitcast.135), calls=%async_computation | async-start | bytes 2097152 | tf_op jit(solution)/shard_map/all_to_all | solution.py:126
  119.3 3.6 copy-start.2
  131.5 31.0 %all-to-all-start.3 = ((bf16[2,16,64,512]{3,2,0,1:T(8,128)(2,1)}), bf16[2,16,64,512]{3,2,0,1:T(8,128)(2,1)}, u32[]{:S(2)}, u32[]{:S(2)}) async-start(bf16[2,16,64,512]{3,2,0,1:T(8,128)(2,1)} %copy.59), calls=%async_computation.3 | async-start | bytes 4194304 | tf_op jit(solution)/shard_map/all_to_all | solution.py:118
  162.5 31.2 %all-to-all-start.1 = ((bf16[2,16,64,512]{3,2,0,1:T(8,128)(2,1)}), bf16[2,16,64,512]{3,2,0,1:T(8,128)(2,1)}, u32[]{:S(2)}, u32[]{:S(2)}) async-start(bf16[2,16,64,512]{3,2,0,1:T(8,128)(2,1)} %copy.51), calls=%async_computation.1 | async-start | bytes 4194304 | tf_op jit(solution)/shard_map/all_to_all | solution.py:127
  169.1 7.0 %copy-start.5 = (bf16[1,2,8,64,512]{4,3,2,1,0:T(8,128)(2,1)}, bf16[1,2,8,64,512]{4,3,2,1,0:T(8,128)(2,1)S(1)}, u32[]{:S(2)}) copy-start(bf16[1,2,8,64,512]{4,3,2,1,0:T(8,128)(2,1)S(1)} %copy.63) | copy-start | bytes 3145732
  209.9 7.0 %copy-start.6 = (bf16[1,2,8,64,512]{4,3,2,1,0:T(8,128)(2,1)S(1)}, bf16[1,2,8,64,512]{4,3,2,1,0:T(8,128)(2,1)}, u32[]{:S(2)}) copy-start(bf16[1,2,8,64,512]{4,3,2,1,0:T(8,128)(2,1)} %copy-done.5) | copy-start | bytes 3145732
  209.9 7.0 %copy-start.11 = (f32[2,512,512]{2,1,0:T(8,128)S(1)}, f32[2,512,512]{2,1,0:T(8,128)}, u32[]{:S(2)}) copy-start(f32[2,512,512]{2,1,0:T(8,128)} %fusion.65) | copy-start | bytes 6291460
  216.9 7.4 %copy-start.4 = (f32[2,512,512]{2,1,0:T(8,128)S(1)}, f32[2,512,512]{2,1,0:T(8,128)}, u32[]{:S(2)}) copy-start(f32[2,512,512]{2,1,0:T(8,128)} %convolution_subtract_fusion) | copy-start | bytes 6291460
  346.5 3.8 %copy-start = (f32[16,64,512]{2,0,1:T(8,128)S(1)}, f32[16,64,512]{2,0,1:T(8,128)}, u32[]{:S(2)}) copy-start(f32[16,64,512]{2,0,1:T(8,128)} %squeeze.35) | copy-start | bytes 6291460
  346.5 3.8 %copy-start.1 = (f32[16,64,512]{2,0,1:T(8,128)S(1)}, f32[16,64,512]{2,0,1:T(8,128)}, u32[]{:S(2)}) copy-start(f32[16,64,512]{2,0,1:T(8,128)} %squeeze.34) | copy-start | bytes 6291460
  351.7 18.4 %copy-start.8 = (f32[512]{0:T(512)S(1)}, f32[512]{0:T(512)}, u32[]{:S(2)}) copy-start(f32[512]{0:T(512)} %param.11) | copy-start | bytes 6148
